TPU v7x, 32 devices: a whole 2x2x4 slice. The times are simulated.
32 devices in a mesh: row: 4 (over z), col: 8 (over y, x, core).
Axes of the slice: x: 2, y: 2, z: 4, core: 2. Of those that a mesh axis runs over, the one named last changes fastest.
Arguments:
- rhs_front: float32 [4, 6144, 1024], P(None, 'row', 'col'), may hold values from -6 to 6
- lower_blocks: float32 [6, 6144, 6144], P(None, 'row', 'col'), may hold values from -0.046875 to 0.046875
- panel_inverse: float32 [4, 6144, 6144], P(None, 'col', 'row'), may hold values from -0.078125 to 0.078125
- child_rows: float32 [4, 64, 128, 1024], P('row', 'col'), may hold values from -4 to 4
- child_map: int32 [4, 64], P('row', 'col'), may hold values from 0 to 47
- child_owner: int32 [8, 24, 1], P('col'), may hold values from 0 to 3; in each aligned block of 24 rows (0 to 23, 24 to 47, ..., all dimensions but the last counted through in order) at most 7 rows name the same one
Outputs:
- solution: float32 [4, 6144, 1024], P(None, 'col')
- child_rhs: float32 [8, 4, 7, 128, 1024], P('col', 'row')
Inputs may be any that keep to these rules, and one draw needn't show every extreme that they name: `child_map`: several child update blocks may name the same front block. `child_owner`: of the 24 solved blocks of one column group, at most 7 name the same row group, and in some column group one row group is named exactly 7 times.
All inputs are finite; a program needn't handle non-finite values.
Results may differ from a plain program's by a relative error of at most 0.00012.
Values sent between devices are 32-bit elements; how exact they have to be, the bound alone decides.
A program may use at most 192 MiB of HBM per device.

v0:
```python
import jax
import jax.numpy as jnp
from jax import lax
from jax.sharding import PartitionSpec as P


def on_device(rhs_front, lower_blocks, panel_inverse, child_rows, child_map, child_owner):
    highest = lax.Precision.HIGHEST
    row_count = lax.axis_size("row")
    row_at = lax.axis_index("row")
    col_at = lax.axis_index("col")
    panels, row_span, narrow = rhs_front.shape
    col_span = panel_inverse.shape[1]
    block = child_rows.shape[2]
    width = child_rows.shape[3]
    local_blocks = panels * row_span // block
    per_panel = col_span // block
    held_blocks = panels * per_panel
    most = max(2, held_blocks // row_count + 1)
    share = width // row_count
    targets = jnp.arange(local_blocks, dtype=jnp.int32)
    picks = (child_map[0][None, :] == targets[:, None]).astype(jnp.float32)
    added = jnp.einsum("lk,kbr->lbr", picks, child_rows[0], precision=highest).reshape(
        panels, row_span, width
    )
    placed = lax.dynamic_update_slice(
        jnp.zeros((panels, row_span, width), jnp.float32), rhs_front, (0, 0, col_at * narrow)
    )
    assembled = added + placed
    owner = child_owner[0, :, 0]
    hits = (owner[None, :] == jnp.arange(row_count, dtype=jnp.int32)[:, None]).astype(jnp.int32)
    ranks = jnp.cumsum(hits, axis=1) - hits
    slot_match = (ranks[:, None, :] == jnp.arange(most, dtype=jnp.int32)[None, :, None]).astype(
        jnp.int32
    )
    routing = (hits[:, None, :] * slot_match).astype(jnp.float32)
    solved = []
    for panel in range(panels):
        front = assembled[panel]
        for prior in range(panel):
            front = front - jnp.dot(
                lower_blocks[panel * (panel - 1) // 2 + prior],
                solved[prior],
                precision=highest,
                preferred_element_type=jnp.float32,
            )
        front = lax.psum(front, "col")
        partial_value = jnp.dot(
            panel_inverse[panel], front, precision=highest, preferred_element_type=jnp.float32
        )
        current = lax.psum(partial_value, "row")
        solved.append(current)
    solution = jnp.stack(solved)
    mine = lax.dynamic_slice_in_dim(
        solution.reshape(held_blocks, block, width), row_at * share, share, 2
    )
    sending = jnp.einsum("dsk,kbr->dsbr", routing, mine, precision=highest)
    received = lax.all_to_all(sending, "row", split_axis=0, concat_axis=3, tiled=True)
    return (solution, received.reshape(1, 1, most, block, width))


def solution(mesh):
    return jax.shard_map(
        on_device,
        mesh=mesh,
        in_specs=(
            P(None, "row", "col"),
            P(None, "row", "col"),
            P(None, "col", "row"),
            P("row", "col", None, None),
            P("row", "col"),
            P("col", None, None),
        ),
        out_specs=(P(None, "col", None), P("col", "row", None, None, None)),
        check_vma=False,
    )
```

profile of v0, /device:TPU:0, one launch (start us, length us, event | category | flops | bytes accessed | tf_op | source)
XLA Modules:
  0.0 1298.2 jit_solution(18290730721862400627)
XLA Ops:
  7.2 0.0 all-reduce.9.cloned.1.call-start
  7.2 16.1 %fusion.38 = f32[48,128,1024]{2,0,1:T(8,128)S(1)} fusion(f32[8,128,1024]{2,1,0:T(8,128)} %bitcast.124, s32[8]{0:T(128)} %bitcast.129), kind=kOutput, calls=%fused_computation.41 | convolution fusion | flops 603980160 | bytes 29360160 | tf_op jit(solution)/shard_map/lk,kbr->lbr/dot_general | solution.py:23
  23.3 27.6 %copy.18 = f32[48,128,1024]{2,1,0:T(8,128)} copy(f32[48,128,1024]{2,0,1:T(8,128)S(1)} %fusion.38) | data formatting | bytes 50331648 | tf_op jit(solution)/shard_map/lk,kbr->lbr/dot_general | solution.py:23
  50.9 25.1 %copy.21 = f32[4,1536,1024]{1,2,0:T(8,128)} copy(f32[4,1536,1024]{2,1,0:T(8,128)} %bitcast.120) | data formatting | bytes 50331648 | tf_op jit(solution)/shard_map/reshape | solution.py:23
  76.0 2.4 copy.20
  78.4 4.1 add_dynamic-update-slice_fusion
  82.5 5.9 slice_bitcast_fusion.3
  88.4 0.0 all-reduce.9.cloned.1.call-update
  88.4 0.0 all-reduce.11.cloned.1.call-start
  88.5 106.8 %all-reduce.9.cloned.1.call-done = f32[1536,1024]{0,1:T(8,128)} async-done(((f32[1536,1024]{0,1:T(8,128)}), f32[1536,1024]{0,1:T(8,128)}) %all-reduce.9.cloned.1.call-update) | async-done | bytes 6291472 | tf_op jit(solution)/shard_map/psum | solution.py:47
  195.3 19.5 %fusion.45 = f32[768,1024]{0,1:T(8,128)} fusion(f32[1536,1024]{0,1:T(8,128)} %all-reduce.9.cloned.1.call-done, f32[4,768,1536]{2,1,0:T(8,128)} %param.8), kind=kOutput, calls=%fused_computation.46 | convolution fusion | flops 14495514624 | bytes 14155776 | tf_op jit(solution)/shard_map/dot_general | solution.py:48
  214.8 0.0 all-reduce.11.cloned.1.call-update
  214.8 0.0 all-reduce.13.cloned.1.call-start
  214.9 121.3 %all-reduce.11.cloned.1.call-done = f32[768,1024]{0,1:T(8,128)} async-done(((f32[768,1024]{0,1:T(8,128)}), f32[768,1024]{0,1:T(8,128)}) %all-reduce.11.cloned.1.call-update) | async-done | bytes 3145744 | tf_op jit(solution)/shard_map/psum | solution.py:51
  336.1 19.6 %fusion.5 = f32[1536,1024]{0,1:T(8,128)} fusion(f32[4,1536,1024]{1,2,0:T(8,128)} %add_dynamic-update-slice_fusion, f32[768,1024]{0,1:T(8,128)} %all-reduce.11.cloned.1.call-done, f32[6,1536,768]{2,1,0:T(8,128)} %param.7), kind=kOutput, calls=%fused_computation.9 | convolution fusion | flops 14497087488 | bytes 20447232 | tf_op jit(solution)/shard_map/dot_general | solution.py:41
  355.8 0.0 all-reduce.13.cloned.1.call-update
  355.8 0.0 all-reduce.15.cloned.1.call-start
  355.8 103.0 %all-reduce.13.cloned.1.call-done = f32[1536,1024]{0,1:T(8,128)} async-done(((f32[1536,1024]{0,1:T(8,128)}), f32[1536,1024]{0,1:T(8,128)}) %all-reduce.13.cloned.1.call-update) | async-done | bytes 6291472 | tf_op jit(solution)/shard_map/psum | solution.py:47
  458.9 19.6 %fusion.48 = f32[768,1024]{0,1:T(8,128)} fusion(f32[1536,1024]{0,1:T(8,128)} %all-reduce.13.cloned.1.call-done, f32[4,768,1536]{2,1,0:T(8,128)} %param.8), kind=kOutput, calls=%fused_computation.47 | convolution fusion | flops 14495514624 | bytes 14155776 | tf_op jit(solution)/shard_map/dot_general | solution.py:48
  478.5 0.0 all-reduce.15.cloned.1.call-update
  478.5 0.0 copy-start
  478.5 0.0 all-reduce.17.cloned.1.call-start
  478.6 121.3 %all-reduce.15.cloned.1.call-done = f32[768,1024]{0,1:T(8,128)} async-done(((f32[768,1024]{0,1:T(8,128)}), f32[768,1024]{0,1:T(8,128)}) %all-reduce.15.cloned.1.call-update) | async-done | bytes 3145744 | tf_op jit(solution)/shard_map/psum | solution.py:51
  599.8 18.3 %fusion.16 = f32[1024,1536]{1,0:T(8,128)S(1)} fusion(f32[768,1024]{0,1:T(8,128)} %all-reduce.15.cloned.1.call-done, f32[6,1536,768]{2,1,0:T(8,128)} %param.7), kind=kOutput, calls=%fused_computation.21 | convolution fusion | flops 14495514624 | bytes 14155776 | tf_op jit(solution)/shard_map/dot_general | solution.py:41
  618.1 0.0 copy-done
  618.1 19.5 %fusion.4 = f32[1536,1024]{0,1:T(8,128)} fusion(f32[4,1536,1024]{1,2,0:T(8,128)} %add_dynamic-update-slice_fusion, f32[1024,1536]{1,0:T(8,128)S(1)} %fusion.16, f32[768,1024]{0,1:T(8,128)S(1)} %copy-done, f32[6,1536,768]{2,1,0:T(8,128)} %param.7), kind=kOutput, calls=%fused_computation.7 | convolution fusion | flops 14498660352 | bytes 26738688 | tf_op jit(solution)/shard_map/dot_general | solution.py:41
  637.6 0.0 all-reduce.17.cloned.1.call-update
  637.7 0.0 all-reduce.19.cloned.1.call-start
  637.7 103.0 %all-reduce.17.cloned.1.call-done = f32[1536,1024]{0,1:T(8,128)} async-done(((f32[1536,1024]{0,1:T(8,128)}), f32[1536,1024]{0,1:T(8,128)}) %all-reduce.17.cloned.1.call-update) | async-done | bytes 6291472 | tf_op jit(solution)/shard_map/psum | solution.py:47
  740.7 19.5 %fusion.51 = f32[768,1024]{0,1:T(8,128)} fusion(f32[1536,1024]{0,1:T(8,128)} %all-reduce.17.cloned.1.call-done, f32[4,768,1536]{2,1,0:T(8,128)} %param.8), kind=kOutput, calls=%fused_computation.48 | convolution fusion | flops 14495514624 | bytes 14155776 | tf_op jit(solution)/shard_map/dot_general | solution.py:48
  760.2 0.0 all-reduce.19.cloned.1.call-update
  760.3 0.0 all-reduce.21.cloned.1.call-start
  760.3 20.1 %fusion.10 = f32[1024,1536]{1,0:T(8,128)} fusion(f32[768,1024]{0,1:T(8,128)} %all-reduce.15.cloned.1.call-done, f32[6,1536,768]{2,1,0:T(8,128)} %param.7), kind=kOutput, calls=%fused_computation.15 | convolution fusion | flops 14495514624 | bytes 14155776 | tf_op jit(solution)/shard_map/dot_general | solution.py:41
  780.4 101.2 %all-reduce.19.cloned.1.call-done = f32[768,1024]{0,1:T(8,128)} async-done(((f32[768,1024]{0,1:T(8,128)}), f32[768,1024]{0,1:T(8,128)}) %all-reduce.19.cloned.1.call-update) | async-done | bytes 3145744 | tf_op jit(solution)/shard_map/psum | solution.py:51
  881.6 0.0 copy-start.1
  881.6 18.8 %fusion.8 = f32[1024,1536]{1,0:T(8,128)S(1)} fusion(f32[768,1024]{0,1:T(8,128)} %all-reduce.19.cloned.1.call-done, f32[6,1536,768]{2,1,0:T(8,128)} %param.7), kind=kOutput, calls=%fused_computation.13 | convolution fusion | flops 14495514624 | bytes 14155776 | tf_op jit(solution)/shard_map/dot_general | solution.py:41
  900.4 0.0 copy-done.1
  900.4 19.7 %fusion.2 = f32[1536,1024]{0,1:T(8,128)} fusion(f32[4,1536,1024]{1,2,0:T(8,128)} %add_dynamic-update-slice_fusion, f32[1024,1536]{1,0:T(8,128)S(1)} %fusion.8, f32[1024,1536]{1,0:T(8,128)S(1)} %copy-done.1, f32[768,1024]{0,1:T(8,128)S(1)} %copy-done, f32[6,1536,768]{2,1,0:T(8,128)} %param.7), kind=kOutput, calls=%fused_computation.4 | convolution fusion | flops 14500233216 | bytes 33030144 | tf_op jit(solution)/shard_map/dot_general | solution.py:41
  920.1 0.0 all-reduce.21.cloned.1.call-update
  920.1 0.0 copy-start.2
  920.1 0.0 all-reduce.23.cloned.1.call-start
  920.2 103.0 %all-reduce.21.cloned.1.call-done = f32[1536,1024]{0,1:T(8,128)} async-done(((f32[1536,1024]{0,1:T(8,128)}), f32[1536,1024]{0,1:T(8,128)}) %all-reduce.21.cloned.1.call-update) | async-done | bytes 6291472 | tf_op jit(solution)/shard_map/psum | solution.py:47
  1023.2 19.7 %fusion.54 = f32[1,768,1024]{1,2,0:T(8,128)} fusion(f32[1536,1024]{0,1:T(8,128)} %all-reduce.21.cloned.1.call-done, f32[4,768,1536]{2,1,0:T(8,128)} %param.8), kind=kOutput, calls=%fused_computation.49 | convolution fusion | flops 14495514624 | bytes 14155776 | tf_op jit(solution)/shard_map/dot_general | solution.py:48
  1042.9 0.0 all-reduce.23.cloned.1.call-update
  1042.9 0.0 copy-done.2
  1042.9 0.2 reduce_window_sum.11
  1043.1 121.1 %all-reduce.23.cloned.1.call-done = f32[1,768,1024]{1,2,0:T(8,128)} async-done(((f32[1,768,1024]{1,2,0:T(8,128)}), f32[1,768,1024]{1,2,0:T(8,128)}) %all-reduce.23.cloned.1.call-update) | async-done | bytes 3145744 | tf_op jit(solution)/shard_map/psum | solution.py:51
  1164.2 9.1 pad_maximum_fusion
  1173.3 12.6 copy.26
  1185.9 2.2 constant_dynamic-slice_fusion
  1188.1 6.7 fusion.44
  1194.8 1.1 copy.24
  1196.0 85.4 %all_to_all.15 = f32[4,7,128,256]{3,2,1,0:T(8,128)} all-to-all(f32[4,7,128,256]{3,2,1,0:T(8,128)S(1)} %copy.24), channel_id=1, replica_groups=mesh['row'=4,'col'=8] {'row'}, dimensions={0} | all-to-all | bytes 7340032 | tf_op jit(solution)/shard_map/all_to_all | solution.py:58
  1281.4 4.6 copy.25
  1286.0 5.0 copy.27
  (2 shorter events, 0.0 us)
Async XLA Ops:
  7.2 188.1 %all-reduce.9.cloned.1.call-start = ((), (), s32[]{:S(2)}) async-start(), calls=%async_computation.1 | async-start | bytes 12582912 | tf_op jit(solution)/shard_map/psum | solution.py:47
  88.4 247.7 %all-reduce.11.cloned.1.call-start = ((), (), s32[]{:S(2)}) async-start(), calls=%async_computation.2 | async-start | bytes 6291456 | tf_op jit(solution)/shard_map/psum | solution.py:51
  214.8 244.0 %all-reduce.13.cloned.1.call-start = ((), (), s32[]{:S(2)}) async-start(), calls=%async_computation.3 | async-start | bytes 12582912 | tf_op jit(solution)/shard_map/psum | solution.py:47
  355.8 244.1 %all-reduce.15.cloned.1.call-start = ((), (), s32[]{:S(2)}) async-start(), calls=%async_computation.4 | async-start | bytes 6291456 | tf_op jit(solution)/shard_map/psum | solution.py:51
  478.5 139.6 %copy-start = (f32[768,1024]{0,1:T(8,128)S(1)}, f32[768,1024]{0,1:T(8,128)}, u32[]{:S(2)}) copy-start(f32[768,1024]{0,1:T(8,128)} %all-reduce.11.cloned.1.call-done) | copy-start | bytes 9437188
  478.5 262.2 %all-reduce.17.cloned.1.call-start = ((), (), s32[]{:S(2)}) async-start(), calls=%async_computation.5 | async-start | bytes 12582912 | tf_op jit(solution)/shard_map/psum | solution.py:47
  637.7 243.9 %all-reduce.19.cloned.1.call-start = ((), (), s32[]{:S(2)}) async-start(), calls=%async_computation.6 | async-start | bytes 6291456 | tf_op jit(solution)/shard_map/psum | solution.py:51
  760.3 262.9 %all-reduce.21.cloned.1.call-start = ((), (), s32[]{:S(2)}) async-start(), calls=%async_computation.7 | async-start | bytes 12582912 | tf_op jit(solution)/shard_map/psum | solution.py:47
  881.6 18.8 %copy-start.1 = (f32[1024,1536]{1,0:T(8,128)S(1)}, f32[1024,1536]{1,0:T(8,128)}, u32[]{:S(2)}) copy-start(f32[1024,1536]{1,0:T(8,128)} %fusion.10) | copy-start | bytes 18874372
  920.1 122.8 %copy-start.2 = (s32[1,24,1]{1,2,0:T(1,128)S(1)}, s32[1,24,1]{1,2,0:T(1,128)}, u32[]{:S(2)}) copy-start(s32[1,24,1]{1,2,0:T(1,128)} %param.11) | copy-start | bytes 292
  920.1 244.1 %all-reduce.23.cloned.1.call-start = ((), (), s32[]{:S(2)}) async-start(), calls=%async_computation.8 | async-start | bytes 6291456 | tf_op jit(solution)/shard_map/psum | solution.py:51
Sparse Core Ops, SparseCore 0:
  88.6 106.6 all-reduce.8
  214.9 121.1 all-reduce.10
  355.9 102.9 all-reduce.12
  478.6 121.1 all-reduce.14
  637.8 102.9 all-reduce.16
  760.4 121.1 all-reduce.18
  920.2 102.8 all-reduce.20
  1043.0 121.1 all-reduce.22
where the time goes:
time: 1310 us; the launch traced here: 1300 us
  waiting for transfers between devices  881 us (67%)
  matrix products  217 us (17%)
  local copies, waits for them, and re-layouts  86.5 us (7%)
  blocking collectives  85.4 us (7%)
  between operations  14.6 us (1%)
  other arithmetic  13.4 us (1%)
    psum x4, waiting for transfers between devices, on_device(): current = lax.psum(partial_value, 'row')  465 us
    psum x4, waiting for transfers between devices, on_device(): front = lax.psum(front, 'col')  416 us
    dot_general x6, matrix products, on_device(): jnp.dot(lower_blocks[panel * (panel - 1) // 2 + prior], solved[prior], pr...  116 us
    all_to_all x1, blocking collectives, on_device(): lax.all_to_all(sending, 'row', split_axis=0, concat_axis=3, tiled=True)  85.4 us
    dot_general x4, matrix products, on_device(): jnp.dot(panel_inverse[panel], front, precision=highest, preferred_element...  78.3 us
    dot_general x1, local copies, waits for them, and re-layouts, on_device(): jnp.einsum('lk,kbr->lbr', picks, child_rows[0], precision=highest)  27.6 us
  transfers between devices with their start and end apart: 8, of which 8 were waited for; matrix products, arithmetic and copies ran while one was open for 2% of the time, Pallas kernels for 0%

commit v1 on v0

--- a/solution.py
+++ b/solution.py
@@ -44,7 +44,9 @@
                 precision=highest,
                 preferred_element_type=jnp.float32,
             )
-        front = lax.psum(front, "col")
+        front = front
+        for hop in (1, 2, 4):
+            front = front + lax.ppermute(front, "col", [(dev, dev ^ hop) for dev in range(8)])
         partial_value = jnp.dot(
             panel_inverse[panel], front, precision=highest, preferred_element_type=jnp.float32
         )

time: 1310 us -> 2050 us (1.56)
  waiting for transfers between devices: 881 us -> 1590 us
  other arithmetic: 13.4 us -> 38.4 us
    ppermute x0 -> x12, waiting for transfers between devices: none -> 1130 us  [on_device(): lax.ppermute(front, 'col', [(dev, dev ^ hop) for dev in range(8)])]
    psum x4 -> x0, waiting for transfers between devices: 416 us -> none  [on_device(): front = lax.psum(front, 'col')]
    add x0 -> x8, other arithmetic: none -> 25 us  [on_device(): front + lax.ppermute(front, 'col', [(dev, dev ^ hop) for dev in range(8)])]
  transfers between devices with their start and end apart: 8 -> 16, of which waited for: 8 -> 16; matrix products, arithmetic and copies ran while one was open for 2% -> 1% of each run, Pallas kernels for 0% -> 0%
where the time goes in v1:
time: 2050 us; the launch traced here: 2040 us
  waiting for transfers between devices  1590 us (78%)
  matrix products  210 us (10%)
  blocking collectives  85.4 us (4%)
  local copies, waits for them, and re-layouts  83.7 us (4%)
  other arithmetic  38.4 us (2%)
    ppermute x12, waiting for transfers between devices, on_device(): lax.ppermute(front, 'col', [(dev, dev ^ hop) for dev in range(8)])  1130 us
    psum x4, waiting for transfers between devices, on_device(): current = lax.psum(partial_value, 'row')  463 us
    dot_general x6, matrix products, on_device(): jnp.dot(lower_blocks[panel * (panel - 1) // 2 + prior], solved[prior], pr...  115 us
    all_to_all x1, blocking collectives, on_device(): lax.all_to_all(sending, 'row', split_axis=0, concat_axis=3, tiled=True)  85.4 us
    dot_general x4, matrix products, on_device(): jnp.dot(panel_inverse[panel], front, precision=highest, preferred_element...  72.6 us
  transfers between devices with their start and end apart: 16, of which 16 were waited for; matrix products, arithmetic and copies ran while one was open for 1% of the time, Pallas kernels for 0%

profile of v1, /device:TPU:0, one launch (start us, length us, event | category | flops | bytes accessed | tf_op | source)
XLA Modules:
  0.0 2036.0 jit_solution(3340305420311828483)
XLA Ops:
  7.2 16.1 fusion.42
  23.3 27.5 %copy.22 = f32[48,128,1024]{2,1,0:T(8,128)} copy(f32[48,128,1024]{2,0,1:T(8,128)S(1)} %fusion.42) | data formatting | bytes 50331648 | tf_op jit(solution)/shard_map/lk,kbr->lbr/dot_general | solution.py:23
  50.8 24.9 %copy.25 = f32[4,1536,1024]{1,2,0:T(8,128)} copy(f32[4,1536,1024]{2,1,0:T(8,128)} %bitcast.118) | data formatting | bytes 50331648 | tf_op jit(solution)/shard_map/reshape | solution.py:23
  75.7 2.4 copy.24
  78.1 4.1 add_dynamic-update-slice_fusion
  82.2 3.2 slice_bitcast_fusion.3
  85.4 0.5 collective-permute-start
  86.0 9.8 collective-permute-done
  95.8 4.2 fusion.81
  99.9 2.9 collective-permute-start.1
  102.9 135.8 %collective-permute-done.1 = f32[1536,1024]{0,1:T(8,128)S(1)} collective-permute-done((f32[1536,1024]{0,1:T(8,128)S(1)}, f32[1536,1024]{0,1:T(8,128)S(1)}, u32[]{:S(2)}, u32[]{:S(2)}) %collective-permute-start.1) | collective-permute-done | bytes 6291488 | tf_op jit(solution)/shard_map/ppermute | solution.py:49
  238.7 1.4 add.57
  240.1 1.9 collective-permute-start.2
  241.9 135.2 %collective-permute-done.2 = f32[1536,1024]{0,1:T(8,128)S(1)} collective-permute-done((f32[1536,1024]{0,1:T(8,128)S(1)}, f32[1536,1024]{0,1:T(8,128)S(1)}, u32[]{:S(2)}, u32[]{:S(2)}) %collective-permute-start.2) | collective-permute-done | bytes 6291488 | tf_op jit(solution)/shard_map/ppermute | solution.py:49
  377.1 18.0 fusion.49
  395.2 0.0 all-reduce.7.cloned.1.call-start
  395.2 122.4 %all-reduce.5.cloned.1.call-done = f32[768,1024]{0,1:T(8,128)} async-done(((f32[768,1024]{0,1:T(8,128)}), f32[768,1024]{0,1:T(8,128)}) %all-reduce.5.cloned.1.call-update) | async-done | bytes 3145744 | tf_op jit(solution)/shard_map/psum | solution.py:53
  517.6 19.5 fusion.5
  537.1 0.1 collective-permute-start.3
  537.2 10.1 collective-permute-done.3
  547.4 1.4 add.59
  548.7 1.5 collective-permute-start.4
  550.3 136.1 %collective-permute-done.4 = f32[1536,1024]{0,1:T(8,128)S(1)} collective-permute-done((f32[1536,1024]{0,1:T(8,128)S(1)}, f32[1536,1024]{0,1:T(8,128)S(1)}, u32[]{:S(2)}, u32[]{:S(2)}) %collective-permute-start.4) | collective-permute-done | bytes 6291488 | tf_op jit(solution)/shard_map/ppermute | solution.py:49
  686.4 1.4 add.60
  687.8 1.5 collective-permute-start.5
  689.3 135.2 %collective-permute-done.5 = f32[1536,1024]{0,1:T(8,128)S(1)} collective-permute-done((f32[1536,1024]{0,1:T(8,128)S(1)}, f32[1536,1024]{0,1:T(8,128)S(1)}, u32[]{:S(2)}, u32[]{:S(2)}) %collective-permute-start.5) | collective-permute-done | bytes 6291488 | tf_op jit(solution)/shard_map/ppermute | solution.py:49
  824.5 18.4 fusion.54
  843.0 0.0 all-reduce.9.cloned.1.call-start
  843.0 120.2 %all-reduce.7.cloned.1.call-done = f32[768,1024]{0,1:T(8,128)} async-done(((f32[768,1024]{0,1:T(8,128)}), f32[768,1024]{0,1:T(8,128)}) %all-reduce.7.cloned.1.call-update) | async-done | bytes 3145744 | tf_op jit(solution)/shard_map/psum | solution.py:53
  963.2 18.3 fusion.22
  981.4 18.8 fusion.4
  1000.2 0.1 collective-permute-start.6
  1000.3 10.3 collective-permute-done.6
  1010.6 4.2 add.62
  1014.8 1.5 collective-permute-start.7
  1016.3 136.2 %collective-permute-done.7 = f32[1536,1024]{0,1:T(8,128)} collective-permute-done((f32[1536,1024]{0,1:T(8,128)S(1)}, f32[1536,1024]{0,1:T(8,128)}, u32[]{:S(2)}, u32[]{:S(2)}) %collective-permute-start.7) | collective-permute-done | bytes 6291488 | tf_op jit(solution)/shard_map/ppermute | solution.py:49
  1152.5 4.2 add.63
  1156.7 1.5 collective-permute-start.8
  1158.2 135.2 %collective-permute-done.8 = f32[1536,1024]{0,1:T(8,128)S(1)} collective-permute-done((f32[1536,1024]{0,1:T(8,128)S(1)}, f32[1536,1024]{0,1:T(8,128)S(1)}, u32[]{:S(2)}, u32[]{:S(2)}) %collective-permute-start.8) | collective-permute-done | bytes 6291488 | tf_op jit(solution)/shard_map/ppermute | solution.py:49
  1293.4 18.0 fusion.59
  1311.5 0.0 all-reduce.11.cloned.1.call-start
  1311.5 19.7 fusion.17
  1331.2 100.5 %all-reduce.9.cloned.1.call-done = f32[768,1024]{0,1:T(8,128)} async-done(((f32[768,1024]{0,1:T(8,128)}), f32[768,1024]{0,1:T(8,128)}) %all-reduce.9.cloned.1.call-update) | async-done | bytes 3145744 | tf_op jit(solution)/shard_map/psum | solution.py:53
  1431.7 19.1 fusion.15
  1450.8 19.6 fusion.2
  1470.4 0.1 collective-permute-start.9
  1470.5 10.3 collective-permute-done.9
  1480.8 4.2 add.65
  1484.9 1.5 collective-permute-start.10
  1486.5 136.2 %collective-permute-done.10 = f32[1536,1024]{0,1:T(8,128)} collective-permute-done((f32[1536,1024]{0,1:T(8,128)S(1)}, f32[1536,1024]{0,1:T(8,128)}, u32[]{:S(2)}, u32[]{:S(2)}) %collective-permute-start.10) | collective-permute-done | bytes 6291488 | tf_op jit(solution)/shard_map/ppermute | solution.py:49
  1622.6 4.2 add.66
  1626.8 1.5 collective-permute-start.11
  1628.4 135.2 %collective-permute-done.11 = f32[1536,1024]{0,1:T(8,128)S(1)} collective-permute-done((f32[1536,1024]{0,1:T(8,128)S(1)}, f32[1536,1024]{0,1:T(8,128)S(1)}, u32[]{:S(2)}, u32[]{:S(2)}) %collective-permute-start.11) | collective-permute-done | bytes 6291488 | tf_op jit(solution)/shard_map/ppermute | solution.py:49
  1763.6 18.2 fusion.64
  1781.9 0.2 reduce_window_sum.11
  1782.1 120.0 %all-reduce.11.cloned.1.call-done = f32[1,768,1024]{1,2,0:T(8,128)} async-done(((f32[1,768,1024]{1,2,0:T(8,128)}), f32[1,768,1024]{1,2,0:T(8,128)}) %all-reduce.11.cloned.1.call-update) | async-done | bytes 3145744 | tf_op jit(solution)/shard_map/psum | solution.py:53
  1902.0 9.1 pad_maximum_fusion
  1911.1 12.8 copy.30
  1924.0 2.2 constant_dynamic-slice_fusion
  1926.2 6.7 fusion.48
  1932.9 1.1 copy.28
  1934.1 85.4 %all_to_all.15 = f32[4,7,128,256]{3,2,1,0:T(8,128)} all-to-all(f32[4,7,128,256]{3,2,1,0:T(8,128)S(1)} %copy.28), channel_id=1, replica_groups=mesh['row'=4,'col'=8] {'row'}, dimensions={0} | all-to-all | bytes 7340032 | tf_op jit(solution)/shard_map/all_to_all | solution.py:60
  2019.4 4.6 copy.29
  2024.0 5.0 copy.31
  (13 shorter events, 0.1 us)
Async XLA Ops:
  7.2 510.4 %all-reduce.5.cloned.1.call-start = ((), (), s32[]{:S(2)}) async-start(), calls=%async_computation.1 | async-start | bytes 6291456 | tf_op jit(solution)/shard_map/psum | solution.py:53
  85.4 10.3 collective-permute-start
  99.9 138.7 %collective-permute-start.1 = (f32[1536,1024]{0,1:T(8,128)S(1)}, f32[1536,1024]{0,1:T(8,128)S(1)}, u32[]{:S(2)}, u32[]{:S(2)}) collective-permute-start(f32[1536,1024]{0,1:T(8,128)S(1)} %fusion.81), channel_id=1, source_target_pairs={{0,2},{1,3},{2,0},{3,1},{4,6},{5,7},{6,4},{7,5},{8,10},{9,11},{10,... | collective-permute-start | bytes 18874376 | tf_op jit(solution)/shard_map/ppermute | solution.py:49
  240.1 137.0 %collective-permute-start.2 = (f32[1536,1024]{0,1:T(8,128)S(1)}, f32[1536,1024]{0,1:T(8,128)S(1)}, u32[]{:S(2)}, u32[]{:S(2)}) collective-permute-start(f32[1536,1024]{0,1:T(8,128)S(1)} %add.57), channel_id=1, source_target_pairs={{0,4},{1,5},{2,6},{3,7},{4,0},{5,1},{6,2},{7,3},{8,12},{9,13},{10,... | collective-permute-start | bytes 18874376 | tf_op jit(solution)/shard_map/ppermute | solution.py:49
  395.2 568.0 %all-reduce.7.cloned.1.call-start = ((), (), s32[]{:S(2)}) async-start(), calls=%async_computation.2 | async-start | bytes 6291456 | tf_op jit(solution)/shard_map/psum | solution.py:53
  537.1 10.2 collective-permute-start.3
  548.7 137.6 %collective-permute-start.4 = (f32[1536,1024]{0,1:T(8,128)S(1)}, f32[1536,1024]{0,1:T(8,128)S(1)}, u32[]{:S(2)}, u32[]{:S(2)}) collective-permute-start(f32[1536,1024]{0,1:T(8,128)S(1)} %add.59), channel_id=1, source_target_pairs={{0,2},{1,3},{2,0},{3,1},{4,6},{5,7},{6,4},{7,5},{8,10},{9,11},{10,... | collective-permute-start | bytes 18874376 | tf_op jit(solution)/shard_map/ppermute | solution.py:49
  687.8 136.8 %collective-permute-start.5 = (f32[1536,1024]{0,1:T(8,128)S(1)}, f32[1536,1024]{0,1:T(8,128)S(1)}, u32[]{:S(2)}, u32[]{:S(2)}) collective-permute-start(f32[1536,1024]{0,1:T(8,128)S(1)} %add.60), channel_id=1, source_target_pairs={{0,4},{1,5},{2,6},{3,7},{4,0},{5,1},{6,2},{7,3},{8,12},{9,13},{10,... | collective-permute-start | bytes 18874376 | tf_op jit(solution)/shard_map/ppermute | solution.py:49
  843.0 138.5 %copy-start = (f32[768,1024]{0,1:T(8,128)S(1)}, f32[768,1024]{0,1:T(8,128)}, u32[]{:S(2)}) copy-start(f32[768,1024]{0,1:T(8,128)} %all-reduce.5.cloned.1.call-done) | copy-start | bytes 9437188
  843.0 588.7 %all-reduce.9.cloned.1.call-start = ((), (), s32[]{:S(2)}) async-start(), calls=%async_computation.3 | async-start | bytes 6291456 | tf_op jit(solution)/shard_map/psum | solution.py:53
  1000.2 10.4 collective-permute-start.6
  1014.8 137.7 %collective-permute-start.7 = (f32[1536,1024]{0,1:T(8,128)S(1)}, f32[1536,1024]{0,1:T(8,128)}, u32[]{:S(2)}, u32[]{:S(2)}) collective-permute-start(f32[1536,1024]{0,1:T(8,128)S(1)} %add.62), channel_id=1, source_target_pairs={{0,2},{1,3},{2,0},{3,1},{4,6},{5,7},{6,4},{7,5},{8,10},{9,11},{10,... | collective-permute-start | bytes 18874376 | tf_op jit(solution)/shard_map/ppermute | solution.py:49
  1156.7 136.8 %collective-permute-start.8 = (f32[1536,1024]{0,1:T(8,128)S(1)}, f32[1536,1024]{0,1:T(8,128)S(1)}, u32[]{:S(2)}, u32[]{:S(2)}) collective-permute-start(f32[1536,1024]{0,1:T(8,128)S(1)} %add.63), channel_id=1, source_target_pairs={{0,4},{1,5},{2,6},{3,7},{4,0},{5,1},{6,2},{7,3},{8,12},{9,13},{10,... | collective-permute-start | bytes 18874376 | tf_op jit(solution)/shard_map/ppermute | solution.py:49
  1311.5 590.6 %all-reduce.11.cloned.1.call-start = ((), (), s32[]{:S(2)}) async-start(), calls=%async_computation.4 | async-start | bytes 6291456 | tf_op jit(solution)/shard_map/psum | solution.py:53
  1431.7 19.1 copy-start.1
  1470.4 10.4 collective-permute-start.9
  1484.9 137.7 %collective-permute-start.10 = (f32[1536,1024]{0,1:T(8,128)S(1)}, f32[1536,1024]{0,1:T(8,128)}, u32[]{:S(2)}, u32[]{:S(2)}) collective-permute-start(f32[1536,1024]{0,1:T(8,128)S(1)} %add.65), channel_id=1, source_target_pairs={{0,2},{1,3},{2,0},{3,1},{4,6},{5,7},{6,4},{7,5},{8,10},{9,11},{10,... | collective-permute-start | bytes 18874376 | tf_op jit(solution)/shard_map/ppermute | solution.py:49
  1626.8 155.0 %copy-start.2 = (s32[1,24,1]{1,2,0:T(1,128)S(1)}, s32[1,24,1]{1,2,0:T(1,128)}, u32[]{:S(2)}) copy-start(s32[1,24,1]{1,2,0:T(1,128)} %param.11) | copy-start | bytes 292
  1626.8 136.8 %collective-permute-start.11 = (f32[1536,1024]{0,1:T(8,128)S(1)}, f32[1536,1024]{0,1:T(8,128)S(1)}, u32[]{:S(2)}, u32[]{:S(2)}) collective-permute-start(f32[1536,1024]{0,1:T(8,128)S(1)} %add.66), channel_id=1, source_target_pairs={{0,4},{1,5},{2,6},{3,7},{4,0},{5,1},{6,2},{7,3},{8,12},{9,13},{10,... | collective-permute-start | bytes 18874376 | tf_op jit(solution)/shard_map/ppermute | solution.py:49
Sparse Core Ops, SparseCore 0:
  395.3 122.2 all-reduce.4
  843.1 120.0 all-reduce.6
  1311.6 120.0 all-reduce.8
  1782.0 120.0 all-reduce.10
